TPU v7x, 32 devices: a whole 2x2x4 slice. The times are simulated.
32 devices in a mesh: dp: 2 (over x), section: 4 (over y, core), tensor: 4 (over z).
Axes of the slice: x: 2, y: 2, z: 4, core: 2. Of those that a mesh axis runs over, the one named last changes fastest.
Arguments:
- block_in: bfloat16 [64, 2, 4096], P('dp', None, 'tensor'), may hold values from -128 to 128
- weights: bfloat16 [12, 2, 4096, 8192], P('section', None, 'tensor', 'dp'), may hold values from -0.0625 to 0.0625
- gains: float32 [12, 2, 4096], P('section', None, 'tensor'), may hold values from 0.1 to 1.9
- layer_counts: int32 [4], replicated, may hold values from 1 to 3, 8 in all
Outputs:
- block_out: bfloat16 [64, 2, 4096], P('dp', None, 'tensor')
- gram_in: float32 [2, 4096, 2, 4096], P(None, 'tensor', 'dp', 'section')
- gram_cross: float32 [2, 4096, 2, 4096], P(None, 'tensor', 'dp', 'section')
Inputs may be any that keep to these rules, and one draw needn't show every extreme that they name: `layer_counts`: each entry is 1 to 3, they sum to 8, and the largest is exactly 3.
All inputs are finite; a program needn't handle non-finite values.
Results may differ from a plain program's by a relative error of at most 0.0093.
Values may be sent and summed in bfloat16 or wider, within the bound.
A program may use at most 192 MiB of HBM per device.

v0:
```python
import jax
import jax.numpy as jnp
from jax import lax
from jax.sharding import PartitionSpec as P

D = 8192
MICRO = 4
SLOTS = 3


EPSILON = 1e-05


def from_behind(block, axis, distance):
    devices = range(lax.axis_size(axis))
    route = [(i - distance, i) for i in devices if i - distance in devices]
    return lax.ppermute(block, axis, route)


def from_root(array, axis, root):
    mine = lax.axis_index(axis) == root
    return lax.psum(jnp.where(mine, array, jnp.zeros_like(array)), axis)


def apply_layer(x_rows, weight, gain_row):
    blocks, quarter, block_cols = weight.shape
    tok_rows = x_rows.shape[0]
    wide_rows = x_rows.astype(jnp.float32)
    squares = lax.psum(jnp.sum(wide_rows * wide_rows, axis=1), "tensor")
    scale = lax.rsqrt(squares / D + EPSILON)
    normed = (wide_rows * scale[:, None] * gain_row.reshape(1, -1)).astype(jnp.bfloat16)
    gathered = lax.all_gather(normed, "dp", axis=0, tiled=True)
    matrix = weight.reshape(blocks * quarter, block_cols)
    all_rows = gathered.shape[0]
    piece_width = block_cols // lax.axis_size("tensor")
    block_count = all_rows * lax.axis_size("tensor") // all_rows
    product = jnp.dot(gathered, matrix, preferred_element_type=jnp.float32)
    product = product.reshape(all_rows, block_count, piece_width).transpose(1, 0, 2)
    summed = lax.psum_scatter(
        product.reshape(block_count * all_rows, piece_width),
        "tensor",
        scatter_dimension=0,
        tiled=True,
    )
    update = summed.astype(jnp.bfloat16).reshape(blocks, tok_rows, 1, piece_width)
    update = lax.all_to_all(update, "dp", split_axis=0, concat_axis=2, tiled=True)
    update = update.reshape(tok_rows, blocks * piece_width)
    return (wide_rows + update.astype(jnp.float32)).astype(jnp.bfloat16)


def local(block_in, weights, gains, layer_counts):
    tok_rows, blocks, quarter = block_in.shape
    micro_rows = tok_rows // MICRO
    features = blocks * quarter
    batches = block_in.reshape(MICRO, micro_rows, features)
    segment_id = lax.axis_index("section")
    segment_count = lax.axis_size("section")
    last_segment = segment_count - 1
    layer_total = layer_counts[segment_id]
    finished = jnp.zeros((MICRO, micro_rows, features), jnp.bfloat16)

    def one_layer(slot_id, current):
        return apply_layer(current, weights[slot_id], gains[slot_id])

    def slot_step(slot_id, current):
        return jnp.where(slot_id < layer_total, one_layer(slot_id, current), current)

    incoming = jnp.zeros((micro_rows, features), jnp.bfloat16)
    step_total = MICRO + segment_count - 1
    for step_id in range(step_total):
        batch_id = step_id - segment_id
        usable = (batch_id >= 0) & (batch_id < MICRO)
        clipped = jnp.clip(batch_id, 0, MICRO - 1)
        current = jnp.where(segment_id == 0, batches[clipped], incoming)
        current = lax.fori_loop(0, SLOTS, slot_step, current)
        storing = usable & (segment_id == last_segment)
        finished = jnp.where(
            storing, lax.dynamic_update_index_in_dim(finished, current, clipped, 0), finished
        )
        if step_id + 1 < step_total:
            incoming = from_behind(current, "section", 1)
    block_out = from_root(finished.reshape(tok_rows, features), "section", last_segment)
    out_blocks = block_out.reshape(tok_rows, blocks, quarter)
    col_in, col_out = (
        lax.all_to_all(block_in, "dp", split_axis=1, concat_axis=0, tiled=True),
        lax.all_to_all(out_blocks, "dp", split_axis=1, concat_axis=0, tiled=True),
    )
    piece_width = quarter * lax.axis_size("tensor") // segment_count
    full_in, full_out = (
        lax.all_gather(col_in, "tensor", axis=2, tiled=True),
        lax.all_gather(col_out, "tensor", axis=2, tiled=True),
    )
    begin = segment_id * piece_width
    cols_in = lax.dynamic_slice_in_dim(full_in[:, 0, :], begin, piece_width, 1)
    cols_out = lax.dynamic_slice_in_dim(full_out[:, 0, :], begin, piece_width, 1)
    contract = (((0,), (0,)), ((), ()))
    rows_local = block_in.reshape(tok_rows, features)
    piece = lax.all_gather(rows_local, "dp", axis=0, tiled=True)
    first_sum = lax.dot_general(piece, cols_in, contract, preferred_element_type=jnp.float32)
    second_sum = lax.dot_general(piece, cols_out, contract, preferred_element_type=jnp.float32)
    token_total = tok_rows * lax.axis_size("dp")
    gram_in = (first_sum / token_total).reshape(blocks, quarter, 1, piece_width)
    gram_cross = (second_sum / token_total).reshape(blocks, quarter, 1, piece_width)
    return (out_blocks, gram_in, gram_cross)


def solution(mesh):
    return jax.shard_map(
        local,
        mesh=mesh,
        in_specs=(
            P("dp", None, "tensor"),
            P("section", None, "tensor", "dp"),
            P("section", None, "tensor"),
            P(),
        ),
        out_specs=(
            P("dp", None, "tensor"),
            P(None, "tensor", "dp", "section"),
            P(None, "tensor", "dp", "section"),
        ),
        check_vma=False,
    )
```

profile of v0, /device:TPU:0, one launch (start us, length us, event | category | flops | bytes accessed | tf_op | source)
XLA Modules:
  0.0 1868.0 jit_solution(9490806258050698548)
XLA Ops:
  9.0 122.3 %copy.38 = bf16[3,2,1024,4096]{2,1,3,0:T(2,128)(2,1)} copy(bf16[3,2,1024,4096]{3,2,1,0:T(8,128)(2,1)} %param.19) | data formatting | bytes 100663296 | tf_op jit(solution)/shard_map/while | solution.py:75
  131.9 227.1 %while.91 = (s32[]{:T(128)}, bf16[8,2048]{1,0:T(8,128)(2,1)S(1)}, s32[]{:T(128)}, f32[3,2,1024]{2,1,0:T(2,128)S(1)}, bf16[3,2,1024,4096]{2,1,3,0:T(2,128)(2,1)}, /*index=5*/s32[]{:T(128)}) while((s32[]{:T(128)}, bf16[8,2048]{1,0:T(8,128)(2,1)S(1)}, s32[]{:T(128)}, f32[3,2,1024]{2,1,0:T(2,128)S(1)}, bf16[3,2,1024,4096]{2,1,3,0:T(2,128)(2,1)}, ...), condition=%wide.region_4.5_spmd, body=%wide.region_0.4_spmd.sunk | while | flops 268648480 | bytes 85860712 | solution.py:75
  132.0 13.2 constant_dynamic-slice_fusion.14
  154.6 13.5 psum.92
  172.7 10.9 fusion.116
  183.7 18.3 reduce-scatter.8.cloned.1.call-done
  210.8 13.2 constant_dynamic-slice_fusion.14
  246.9 10.9 fusion.116
  257.8 18.4 reduce-scatter.8.cloned.1.call-done
  284.9 13.2 constant_dynamic-slice_fusion.14
  331.9 18.5 reduce-scatter.8.cloned.1.call-done
  367.1 222.9 %while.92 = (s32[]{:T(128)}, bf16[8,2048]{1,0:T(8,128)(2,1)S(1)}, s32[]{:T(128)}, f32[3,2,1024]{2,1,0:T(2,128)S(1)}, bf16[3,2,1024,4096]{2,1,3,0:T(2,128)(2,1)}, /*index=5*/s32[]{:T(128)}) while((s32[]{:T(128)}, bf16[8,2048]{1,0:T(8,128)(2,1)S(1)}, s32[]{:T(128)}, f32[3,2,1024]{2,1,0:T(2,128)S(1)}, bf16[3,2,1024,4096]{2,1,3,0:T(2,128)(2,1)}, ...), condition=%wide.region_9.10_spmd, body=%wide.region_5.9_spmd.sunk | while | flops 268648480 | bytes 85860712 | solution.py:75
  367.2 13.2 constant_dynamic-slice_fusion.15
  414.1 18.9 %reduce-scatter.10.cloned.1.call-done = f32[16,1024]{1,0:T(8,128)} async-done(((f32[64,1024]{1,0:T(8,128)}), f32[16,1024]{1,0:T(8,128)}) %reduce-scatter.10.cloned.1.call-update) | async-done | bytes 65552 | tf_op jit(solution)/shard_map/while/body/eval_jaxpr/reduce_scatter | solution.py:39
  441.8 13.2 constant_dynamic-slice_fusion.15
  477.8 10.9 fusion.122
  488.7 18.5 reduce-scatter.10.cloned.1.call-done
  515.9 13.2 constant_dynamic-slice_fusion.15
  551.9 10.9 fusion.122
  562.9 18.5 reduce-scatter.10.cloned.1.call-done
  592.2 225.5 %while.93 = (s32[]{:T(128)}, bf16[8,2048]{1,0:T(8,128)(2,1)S(1)}, s32[]{:T(128)}, f32[3,2,1024]{2,1,0:T(2,128)S(1)}, bf16[3,2,1024,4096]{2,1,3,0:T(2,128)(2,1)}, /*index=5*/s32[]{:T(128)}) while((s32[]{:T(128)}, bf16[8,2048]{1,0:T(8,128)(2,1)S(1)}, s32[]{:T(128)}, f32[3,2,1024]{2,1,0:T(2,128)S(1)}, bf16[3,2,1024,4096]{2,1,3,0:T(2,128)(2,1)}, ...), condition=%wide.region_14.15_spmd, body=%wide.region_10.14_spmd.sunk | while | flops 268648480 | bytes 85860712 | solution.py:75
  592.2 13.2 constant_dynamic-slice_fusion.16
  639.2 21.5 %reduce-scatter.12.cloned.1.call-done = f32[16,1024]{1,0:T(8,128)} async-done(((f32[64,1024]{1,0:T(8,128)}), f32[16,1024]{1,0:T(8,128)}) %reduce-scatter.12.cloned.1.call-update) | async-done | bytes 65552 | tf_op jit(solution)/shard_map/while/body/eval_jaxpr/reduce_scatter | solution.py:39
  669.4 13.2 constant_dynamic-slice_fusion.16
  716.4 18.5 reduce-scatter.12.cloned.1.call-done
  743.6 13.2 constant_dynamic-slice_fusion.16
  790.5 18.5 reduce-scatter.12.cloned.1.call-done
  819.8 225.6 %while.94 = (s32[]{:T(128)}, bf16[8,2048]{1,0:T(8,128)(2,1)S(1)}, s32[]{:T(128)}, f32[3,2,1024]{2,1,0:T(2,128)S(1)}, bf16[3,2,1024,4096]{2,1,3,0:T(2,128)(2,1)}, /*index=5*/s32[]{:T(128)}) while((s32[]{:T(128)}, bf16[8,2048]{1,0:T(8,128)(2,1)S(1)}, s32[]{:T(128)}, f32[3,2,1024]{2,1,0:T(2,128)S(1)}, bf16[3,2,1024,4096]{2,1,3,0:T(2,128)(2,1)}, ...), condition=%wide.region_19.20_spmd, body=%wide.region_15.19_spmd.sunk | while | flops 268648480 | bytes 85860712 | solution.py:75
  819.9 13.2 constant_dynamic-slice_fusion.17
  866.8 21.6 %reduce-scatter.14.cloned.1.call-done = f32[16,1024]{1,0:T(8,128)} async-done(((f32[64,1024]{1,0:T(8,128)}), f32[16,1024]{1,0:T(8,128)}) %reduce-scatter.14.cloned.1.call-update) | async-done | bytes 65552 | tf_op jit(solution)/shard_map/while/body/eval_jaxpr/reduce_scatter | solution.py:39
  897.1 13.2 constant_dynamic-slice_fusion.17
  944.1 18.4 reduce-scatter.14.cloned.1.call-done
  971.3 13.2 constant_dynamic-slice_fusion.17
  1007.3 10.9 fusion.134
  1018.2 18.5 reduce-scatter.14.cloned.1.call-done
  1047.6 225.5 %while.95 = (s32[]{:T(128)}, bf16[8,2048]{1,0:T(8,128)(2,1)S(1)}, s32[]{:T(128)}, f32[3,2,1024]{2,1,0:T(2,128)S(1)}, bf16[3,2,1024,4096]{2,1,3,0:T(2,128)(2,1)}, /*index=5*/s32[]{:T(128)}) while((s32[]{:T(128)}, bf16[8,2048]{1,0:T(8,128)(2,1)S(1)}, s32[]{:T(128)}, f32[3,2,1024]{2,1,0:T(2,128)S(1)}, bf16[3,2,1024,4096]{2,1,3,0:T(2,128)(2,1)}, ...), condition=%wide.region_24.25_spmd, body=%wide.region_20.24_spmd.sunk | while | flops 268648480 | bytes 85860712 | solution.py:75
  1047.6 13.2 constant_dynamic-slice_fusion.18
  1094.5 21.6 %reduce-scatter.16.cloned.1.call-done = f32[16,1024]{1,0:T(8,128)} async-done(((f32[64,1024]{1,0:T(8,128)}), f32[16,1024]{1,0:T(8,128)}) %reduce-scatter.16.cloned.1.call-update) | async-done | bytes 65552 | tf_op jit(solution)/shard_map/while/body/eval_jaxpr/reduce_scatter | solution.py:39
  1124.8 13.2 constant_dynamic-slice_fusion.18
  1171.8 18.5 reduce-scatter.16.cloned.1.call-done
  1199.0 13.2 constant_dynamic-slice_fusion.18
  1245.9 18.4 reduce-scatter.16.cloned.1.call-done
  1275.2 225.6 %while.96 = (s32[]{:T(128)}, bf16[8,2048]{1,0:T(8,128)(2,1)S(1)}, s32[]{:T(128)}, f32[3,2,1024]{2,1,0:T(2,128)S(1)}, bf16[3,2,1024,4096]{2,1,3,0:T(2,128)(2,1)}, /*index=5*/s32[]{:T(128)}) while((s32[]{:T(128)}, bf16[8,2048]{1,0:T(8,128)(2,1)S(1)}, s32[]{:T(128)}, f32[3,2,1024]{2,1,0:T(2,128)S(1)}, bf16[3,2,1024,4096]{2,1,3,0:T(2,128)(2,1)}, ...), condition=%wide.region_29.30_spmd, body=%wide.region_25.29_spmd.sunk | while | flops 268648480 | bytes 85860712 | solution.py:75
  1275.3 13.2 constant_dynamic-slice_fusion.19
  1322.2 21.6 %reduce-scatter.18.cloned.1.call-done = f32[16,1024]{1,0:T(8,128)} async-done(((f32[64,1024]{1,0:T(8,128)}), f32[16,1024]{1,0:T(8,128)}) %reduce-scatter.18.cloned.1.call-update) | async-done | bytes 65552 | tf_op jit(solution)/shard_map/while/body/eval_jaxpr/reduce_scatter | solution.py:39
  1352.5 13.2 constant_dynamic-slice_fusion.19
  1399.5 18.4 reduce-scatter.18.cloned.1.call-done
  1426.6 13.2 constant_dynamic-slice_fusion.19
  1462.7 10.9 fusion.146
  1473.6 18.5 reduce-scatter.18.cloned.1.call-done
  1502.9 225.5 %while.97 = (s32[]{:T(128)}, bf16[8,2048]{1,0:T(8,128)(2,1)S(1)}, s32[]{:T(128)}, f32[3,2,1024]{2,1,0:T(2,128)S(1)}, bf16[3,2,1024,4096]{2,1,3,0:T(2,128)(2,1)}, /*index=5*/s32[]{:T(128)}) while((s32[]{:T(128)}, bf16[8,2048]{1,0:T(8,128)(2,1)S(1)}, s32[]{:T(128)}, f32[3,2,1024]{2,1,0:T(2,128)S(1)}, bf16[3,2,1024,4096]{2,1,3,0:T(2,128)(2,1)}, ...), condition=%wide.region_34.35_spmd, body=%wide.region_30.34_spmd.sunk | while | flops 268648480 | bytes 85860712 | solution.py:75
  1503.0 13.2 constant_dynamic-slice_fusion.20
  1549.9 21.5 %reduce-scatter.20.cloned.1.call-done = f32[16,1024]{1,0:T(8,128)} async-done(((f32[64,1024]{1,0:T(8,128)}), f32[16,1024]{1,0:T(8,128)}) %reduce-scatter.20.cloned.1.call-update) | async-done | bytes 65552 | tf_op jit(solution)/shard_map/while/body/eval_jaxpr/reduce_scatter | solution.py:39
  1580.2 13.2 constant_dynamic-slice_fusion.20
  1627.2 18.5 reduce-scatter.20.cloned.1.call-done
  1654.4 13.2 constant_dynamic-slice_fusion.20
  1701.4 18.3 reduce-scatter.20.cloned.1.call-done
  1736.3 16.0 all_gather.58
  1752.3 13.3 all-reduce.2.cloned.1.call-done
  1775.2 11.7 reshape.258
  1787.0 20.5 %copy.47 = f32[2,1024,1,1024]{3,2,1,0:T(1,128)} copy(f32[2,1024,1,1024]{1,0,3,2:T(2,128)} %reshape.258) | data formatting | bytes 16777216
  1807.5 15.0 all_gather.60
  1827.2 11.8 reshape.259
  1839.0 20.5 %copy.48 = f32[2,1024,1,1024]{3,2,1,0:T(1,128)} copy(f32[2,1024,1,1024]{1,0,3,2:T(2,128)} %reshape.259) | data formatting | bytes 16777216
  (383 shorter events, 846.6 us)
Async XLA Ops:
  9.0 122.3 %copy-start.4 = (s32[4]{0:T(128)S(1)}, s32[4]{0:T(128)}, u32[]{:S(2)}) copy-start(s32[4]{0:T(128)} %param.21) | copy-start | bytes 52
  9.0 122.9 %copy-start = (f32[3,2,1024]{2,1,0:T(2,128)S(1)}, f32[3,2,1024]{2,1,0:T(2,128)}, u32[]{:S(2)}) copy-start(f32[3,2,1024]{2,1,0:T(2,128)} %param.20) | copy-start | bytes 73732
  131.9 228.5 %copy-start.2 = (bf16[32,2,1024]{2,1,0:T(2,128)(2,1)S(1)}, bf16[32,2,1024]{2,1,0:T(2,128)(2,1)}, u32[]{:S(2)}) copy-start(bf16[32,2,1024]{2,1,0:T(2,128)(2,1)} %param.18) | copy-start | bytes 393220
  132.0 70.1 %reduce-scatter.8.cloned.1.call-start = ((), (), s32[]{:S(2)}) async-start(), calls=%async_computation.17 | async-start | bytes 327680 | tf_op jit(solution)/shard_map/while/body/eval_jaxpr/reduce_scatter | solution.py:39
  203.5 7.2 all-to-all-start
  210.7 65.5 %reduce-scatter.8.cloned.1.call-start = ((), (), s32[]{:S(2)}) async-start(), calls=%async_computation.17 | async-start | bytes 327680 | tf_op jit(solution)/shard_map/while/body/eval_jaxpr/reduce_scatter | solution.py:39
  277.7 7.2 all-to-all-start
  284.9 65.5 %reduce-scatter.8.cloned.1.call-start = ((), (), s32[]{:S(2)}) async-start(), calls=%async_computation.17 | async-start | bytes 327680 | tf_op jit(solution)/shard_map/while/body/eval_jaxpr/reduce_scatter | solution.py:39
  351.8 7.2 all-to-all-start
  359.1 8.0 collective-permute-start
  367.1 65.9 %reduce-scatter.10.cloned.1.call-start = ((), (), s32[]{:S(2)}) async-start(), calls=%async_computation.18 | async-start | bytes 327680 | tf_op jit(solution)/shard_map/while/body/eval_jaxpr/reduce_scatter | solution.py:39
  434.5 7.2 all-to-all-start.1
  441.7 65.5 %reduce-scatter.10.cloned.1.call-start = ((), (), s32[]{:S(2)}) async-start(), calls=%async_computation.18 | async-start | bytes 327680 | tf_op jit(solution)/shard_map/while/body/eval_jaxpr/reduce_scatter | solution.py:39
  508.6 7.2 all-to-all-start.1
  515.9 65.5 %reduce-scatter.10.cloned.1.call-start = ((), (), s32[]{:S(2)}) async-start(), calls=%async_computation.18 | async-start | bytes 327680 | tf_op jit(solution)/shard_map/while/body/eval_jaxpr/reduce_scatter | solution.py:39
  582.8 7.2 all-to-all-start.1
  590.0 2.1 collective-permute-start.1
  592.2 68.5 %reduce-scatter.12.cloned.1.call-start = ((), (), s32[]{:S(2)}) async-start(), calls=%async_computation.19 | async-start | bytes 327680 | tf_op jit(solution)/shard_map/while/body/eval_jaxpr/reduce_scatter | solution.py:39
  662.2 7.2 all-to-all-start.2
  669.4 65.5 %reduce-scatter.12.cloned.1.call-start = ((), (), s32[]{:S(2)}) async-start(), calls=%async_computation.19 | async-start | bytes 327680 | tf_op jit(solution)/shard_map/while/body/eval_jaxpr/reduce_scatter | solution.py:39
  736.3 7.2 all-to-all-start.2
  743.5 65.5 %reduce-scatter.12.cloned.1.call-start = ((), (), s32[]{:S(2)}) async-start(), calls=%async_computation.19 | async-start | bytes 327680 | tf_op jit(solution)/shard_map/while/body/eval_jaxpr/reduce_scatter | solution.py:39
  810.5 7.2 all-to-all-start.2
  817.7 2.1 collective-permute-start.2
  819.8 68.6 %reduce-scatter.14.cloned.1.call-start = ((), (), s32[]{:S(2)}) async-start(), calls=%async_computation.20 | async-start | bytes 327680 | tf_op jit(solution)/shard_map/while/body/eval_jaxpr/reduce_scatter | solution.py:39
  889.9 7.2 all-to-all-start.3
  897.1 65.4 %reduce-scatter.14.cloned.1.call-start = ((), (), s32[]{:S(2)}) async-start(), calls=%async_computation.20 | async-start | bytes 327680 | tf_op jit(solution)/shard_map/while/body/eval_jaxpr/reduce_scatter | solution.py:39
  964.0 7.2 all-to-all-start.3
  971.2 65.5 %reduce-scatter.14.cloned.1.call-start = ((), (), s32[]{:S(2)}) async-start(), calls=%async_computation.20 | async-start | bytes 327680 | tf_op jit(solution)/shard_map/while/body/eval_jaxpr/reduce_scatter | solution.py:39
  1038.2 7.2 all-to-all-start.3
  1045.4 2.1 collective-permute-start.3
  1047.6 68.5 %reduce-scatter.16.cloned.1.call-start = ((), (), s32[]{:S(2)}) async-start(), calls=%async_computation.21 | async-start | bytes 327680 | tf_op jit(solution)/shard_map/while/body/eval_jaxpr/reduce_scatter | solution.py:39
  1117.6 7.2 all-to-all-start.4
  1124.8 65.5 %reduce-scatter.16.cloned.1.call-start = ((), (), s32[]{:S(2)}) async-start(), calls=%async_computation.21 | async-start | bytes 327680 | tf_op jit(solution)/shard_map/while/body/eval_jaxpr/reduce_scatter | solution.py:39
  1191.7 7.2 all-to-all-start.4
  1198.9 65.4 %reduce-scatter.16.cloned.1.call-start = ((), (), s32[]{:S(2)}) async-start(), calls=%async_computation.21 | async-start | bytes 327680 | tf_op jit(solution)/shard_map/while/body/eval_jaxpr/reduce_scatter | solution.py:39
  1265.8 7.2 all-to-all-start.4
  1273.1 2.1 collective-permute-start.4
  1275.2 68.6 %reduce-scatter.18.cloned.1.call-start = ((), (), s32[]{:S(2)}) async-start(), calls=%async_computation.22 | async-start | bytes 327680 | tf_op jit(solution)/shard_map/while/body/eval_jaxpr/reduce_scatter | solution.py:39
  1345.2 7.2 all-to-all-start.5
  1352.5 65.4 %reduce-scatter.18.cloned.1.call-start = ((), (), s32[]{:S(2)}) async-start(), calls=%async_computation.22 | async-start | bytes 327680 | tf_op jit(solution)/shard_map/while/body/eval_jaxpr/reduce_scatter | solution.py:39
  1419.3 7.2 all-to-all-start.5
  1426.6 65.5 %reduce-scatter.18.cloned.1.call-start = ((), (), s32[]{:S(2)}) async-start(), calls=%async_computation.22 | async-start | bytes 327680 | tf_op jit(solution)/shard_map/while/body/eval_jaxpr/reduce_scatter | solution.py:39
  1493.6 7.2 all-to-all-start.5
  1500.8 2.1 collective-permute-start.5
  1502.9 267.6 %copy-start.1 = (bf16[64,2048]{1,0:T(8,128)(2,1)S(1)}, bf16[64,2048]{1,0:T(8,128)(2,1)}, u32[]{:S(2)}) copy-start(bf16[64,2048]{1,0:T(8,128)(2,1)} %all_gather.59) | copy-start | bytes 786436
  1502.9 68.5 %reduce-scatter.20.cloned.1.call-start = ((), (), s32[]{:S(2)}) async-start(), calls=%async_computation.23 | async-start | bytes 327680 | tf_op jit(solution)/shard_map/while/body/eval_jaxpr/reduce_scatter | solution.py:39
  1572.9 7.2 all-to-all-start.6
  1580.2 65.5 %reduce-scatter.20.cloned.1.call-start = ((), (), s32[]{:S(2)}) async-start(), calls=%async_computation.23 | async-start | bytes 327680 | tf_op jit(solution)/shard_map/while/body/eval_jaxpr/reduce_scatter | solution.py:39
  1647.1 7.2 all-to-all-start.6
  1654.3 65.4 %reduce-scatter.20.cloned.1.call-start = ((), (), s32[]{:S(2)}) async-start(), calls=%async_computation.23 | async-start | bytes 327680 | tf_op jit(solution)/shard_map/while/body/eval_jaxpr/reduce_scatter | solution.py:39
  1721.2 7.2 all-to-all-start.6
  1728.4 7.9 all-to-all-start.7
  1731.8 33.8 %all-reduce.2.cloned.1.call-start = ((), (), s32[]{:S(2)}) async-start(), calls=%async_computation.16 | async-start | bytes 262144 | tf_op jit(solution)/shard_map/psum | solution.py:22
  1767.2 40.3 %all-to-all-start.8 = ((bf16[32,2,1024]{2,0,1:T(8,128)(2,1)}), bf16[32,2,1024]{2,0,1:T(8,128)(2,1)S(1)}, u32[]{:S(2)}, u32[]{:S(2)}) async-start(bf16[32,2,1024]{2,0,1:T(8,128)(2,1)} %copy.46), calls=%async_computation.15 | async-start | bytes 262144 | tf_op jit(solution)/shard_map/all_to_all | solution.py:86
  1827.2 32.3 %copy-start.3 = (bf16[32,2,1024]{2,1,0:T(2,128)(2,1)S(1)}, bf16[32,2,1024]{2,1,0:T(2,128)(2,1)}, u32[]{:S(2)}) copy-start(bf16[32,2,1024]{2,1,0:T(2,128)(2,1)} %all-reduce.2.cloned.1.call-done) | copy-start | bytes 393220
Sparse Core Ops, SparseCore 0:
  183.8 18.1 reduce-scatter.7
  257.9 18.2 reduce-scatter.7
  332.0 18.3 reduce-scatter.7
  414.2 18.7 reduce-scatter.9
  488.8 18.2 reduce-scatter.9
  563.0 18.2 reduce-scatter.9
  639.3 21.3 reduce-scatter.11
  716.5 18.2 reduce-scatter.11
  790.7 18.2 reduce-scatter.11
  866.9 21.3 reduce-scatter.13
  944.2 18.2 reduce-scatter.13
  1018.4 18.3 reduce-scatter.13
  1094.7 21.3 reduce-scatter.15
  1171.9 18.2 reduce-scatter.15
  1246.1 18.2 reduce-scatter.15
  1322.3 21.3 reduce-scatter.17
  1399.6 18.2 reduce-scatter.17
  1473.7 18.3 reduce-scatter.17
  1550.0 21.3 reduce-scatter.19
  1627.3 18.2 reduce-scatter.19
  1701.5 18.1 reduce-scatter.19
Sparse Core Ops, SparseCore 1:
  1735.2 30.3 all-reduce.1
where the time goes:
time: 1880 us; the launch traced here: 1870 us
  local copies, waits for them, and re-layouts  664 us (35%)
  waiting for transfers between devices  493 us (26%)
  blocking collectives  322 us (17%)
  matrix products  239 us (13%)
  starting transfers between devices  84.5 us (4%)
  other arithmetic  35.8 us (2%)
    reduce_scatter x21, waiting for transfers between devices, apply_layer(): lax.psum_scatter(product.reshape(block_count * all_rows, piece_width), 't...  403 us
    dynamic_slice x21, local copies, waits for them, and re-layouts, one_layer(): return apply_layer(current, weights[slot_id], gains[slot_id])  278 us
    dot_general x21, matrix products, apply_layer(): product = jnp.dot(gathered, matrix, preferred_element_type=jnp.float32)  229 us
    while x63, local copies, waits for them, and re-layouts  194 us
    psum x21, blocking collectives, apply_layer(): squares = lax.psum(jnp.sum(wide_rows * wide_rows, axis=1), 'tensor')  189 us
    while x1, local copies, waits for them, and re-layouts, local(): current = lax.fori_loop(0, SLOTS, slot_step, current)  122 us
    all_gather x21, blocking collectives, apply_layer(): gathered = lax.all_gather(normed, 'dp', axis=0, tiled=True)  96.1 us
    all_to_all x21, waiting for transfers between devices, apply_layer(): lax.all_to_all(update, 'dp', split_axis=0, concat_axis=2, tiled=True)  69.4 us
  transfers between devices with their start and end apart: 51, of which 49 were waited for; matrix products, arithmetic and copies ran while one was open for 2% of the time, Pallas kernels for 0%

commit v1 on v0

v1 whole, which is shorter than its diff:
```python
import functools

import jax
import jax.numpy as jnp
from jax import lax
from jax.experimental import pallas as pl
from jax.experimental.pallas import tpu as pltpu
from jax.sharding import PartitionSpec as P

LAYERS = 8
EPSILON = 1e-05
MESH = pl.DeviceIdType.MESH
VMEM_LIMIT = 67043328


def windows(ns, slots):
    first = [max(s, LAYERS - slots * (ns - s)) for s in range(ns)]
    last = [min(slots * s, LAYERS - (ns - s)) for s in range(ns)] + [LAYERS]
    return first, last[:ns], last[1:]


def pick(index, values):
    out = jnp.int32(values[0])
    for i in range(1, len(values)):
        out = jnp.where(index == i, jnp.int32(values[i]), out)
    return out


def among(index, members):
    out = index == members[0]
    for m in members[1:]:
        out = out | (index == m)
    return out


def relay(
    nd, ns, nt, slots,
    counts, bi, gains, w_hbm,
    rows_out, cin_out, cout_out, bo_out,
    wv, x0r, xr, hr, hst, xs, xg, ps, pr, own, sss, ssr, cin, fin, cout, bo,
    w_sem, x0_ss, x0_rs, ci_ss, ci_rs, ps_ss, pr_rs, ss_ss, ss_rs, xs_ss, xr_rs, h_ss, h_rs,
    co_ss, co_rs, bo_ss, bo_rs,
):
    nb, tl, q = bi.shape
    T = tl * nd
    tn = min(256, q)
    d, s, t = lax.axis_index("dp"), lax.axis_index("section"), lax.axis_index("tensor")
    first, last, end = windows(ns, slots)

    def tq_of(r):
        return lax.rem(t + r, nt)

    def dp_of(k):
        return lax.rem(d + k, nd)

    def wcopy(k, r):
        cols = pl.ds(pl.multiple_of(tq_of(r) * q, q), q)
        return pltpu.make_async_copy(w_hbm.at[k, :, cols], wv.at[k, :, cols], w_sem.at[k, r - 1])

    def rcopy(src, dst, ss, rs, **to):
        return pltpu.make_async_remote_copy(
            src_ref=src, dst_ref=dst, send_sem=ss, recv_sem=rs,
            device_id={"dp": d, "section": s, "tensor": t, **to}, device_id_type=MESH,
        )

    for k in range(slots):
        for r in range(1, nt + 1):
            wcopy(k, r).start()

    total = nd * ns * nt
    me = (d * ns + s) * nt + t
    barrier = pltpu.get_barrier_semaphore()

    def greet(k, carry):
        o = lax.rem(me + k, total)
        pl.semaphore_signal(
            barrier, inc=1,
            device_id={
                "dp": lax.div(o, ns * nt),
                "section": lax.rem(lax.div(o, nt), ns),
                "tensor": lax.rem(o, nt),
            },
            device_id_type=MESH,
        )
        return carry

    lax.fori_loop(1, total, greet, 0)
    pl.semaphore_wait(barrier, total - 1)

    mine = pl.ds(pl.multiple_of(d * tl, tl), tl)

    def x0copy(k):
        return rcopy(bi, x0r.at[:, mine, :], x0_ss.at[k - 1], x0_rs.at[k - 1], dp=dp_of(k))

    for k in range(1, nd):
        x0copy(k).start()
    x0r[:, mine, :] = bi[...]

    def cicopy(kt, kd):
        to = dp_of(kd)
        return rcopy(
            bi.at[to], cin.at[mine, :], ci_ss, ci_rs.at[kd], dp=to, tensor=tq_of(kt)
        )

    pairs = [(kt, kd) for kt in range(nt) for kd in range(nd) if kt or kd]

    @pl.when(t == s)
    def _():
        for kt, kd in pairs:
            cicopy(kt, kd).start()
        cin[mine, :] = bi[d]

    for k in range(1, nd):
        x0copy(k).wait()

    start = jnp.int32(0)
    for i in range(ns - 1):
        start = start + jnp.where(s > i, counts[i], 0)
    first_s = pick(s, first)
    waited = {i: set() for i in range(ns)}

    def need(j, act):
        spans = {
            i: (max(0, j - last[i]), min(slots - 1, j - first[i])) for i in act
        }
        if all(lo == hi for lo, hi in spans.values()):
            return pick(s, [spans[i][0] if i in spans else 0 for i in range(ns)]), {
                i: {spans[i][0]} for i in act
            }
        return jnp.clip(j - start, 0, slots - 1), {i: set(range(slots)) for i in act}

    def layer(j):
        act = [i for i in range(ns) if first[i] <= j < end[i]]
        par, nxt = j % 2, (j + 1) % 2
        slot, wants = need(j, act)
        takers = [i for i in act if i >= 1 and first[i] <= j <= last[i]]
        fresh = {}
        for i in act:
            fresh[i] = sorted(wants[i] - waited[i])
            waited[i] |= wants[i]

        @pl.when(among(s, act))
        def _():
            hand_id = jnp.clip(j - first_s, 0, hr.shape[0] - 1)
            if takers:
                @pl.when(among(s, takers))
                def _():
                    for kd in range(nd):
                        rcopy(
                            hst.at[0], hr.at[hand_id, 0], h_ss.at[0, kd], h_rs.at[hand_id, kd]
                        ).wait_recv()
                take = among(s, takers) & ((start == j) | (first_s == j))
            gain = gains[slot]
            squares = jnp.zeros((T, 1), jnp.float32)
            for b in range(nb):
                if j == 0:
                    v = x0r[b].astype(jnp.float32)
                elif takers:
                    v = jnp.where(
                        take, hr[hand_id, b].astype(jnp.float32), xr[par, b].astype(jnp.float32)
                    )
                else:
                    v = xr[par, b].astype(jnp.float32)
                xs[b] = v.astype(jnp.bfloat16)
                xg[:, b * q:(b + 1) * q] = (v * gain[:, b * q:(b + 1) * q]).astype(jnp.bfloat16)
                squares = squares + jnp.sum(v * v, axis=1, keepdims=True)
            sss[...] = jnp.broadcast_to(squares, sss.shape)

            def sscopy(r):
                return rcopy(
                    sss, ssr.at[par, r - 1], ss_ss.at[r - 1], ss_rs.at[par, r - 1], tensor=tq_of(r)
                )

            def pscopy(r):
                return rcopy(
                    ps.at[r - 1], pr.at[par, r - 1], ps_ss.at[r - 1], pr_rs.at[par, r - 1],
                    tensor=tq_of(r),
                )

            for r in range(1, nt):
                sscopy(r).start()
            for r in range(1, nt + 1):
                for i in act:
                    if fresh[i]:
                        @pl.when(s == i)
                        def _(i=i):
                            for k in fresh[i]:
                                if r == 1 and len(fresh[i]) > 1:
                                    for rr in range(1, nt + 1):
                                        wcopy(k, rr).wait()
                                elif len(fresh[i]) == 1 and len(wants[i]) == 1:
                                    wcopy(k, r).wait()
                                elif r == 1:
                                    for rr in range(1, nt + 1):
                                        wcopy(k, rr).wait()
                base = tq_of(r) * q

                def tile(i, carry):
                    cols = pl.ds(pl.multiple_of(base + i * tn, tn), tn)
                    acc = jnp.dot(
                        xg[...], wv[slot, :, cols], preferred_element_type=jnp.float32
                    )
                    here = pl.ds(pl.multiple_of(i * tn, tn), tn)
                    if r < nt:
                        ps[r - 1, :, here] = acc.astype(jnp.bfloat16)
                    else:
                        own[:, here] = acc
                    return carry

                lax.fori_loop(0, q // tn, tile, 0)
                if r < nt:
                    pscopy(r).start()
            for r in range(1, nt):
                sscopy(r).wait()
                squares = squares + ssr[par, r - 1][:, :1]
            scale = lax.rsqrt(squares / (nb * q * nt) + EPSILON)
            for r in range(1, nt):
                pscopy(r).wait()
            summed = own[...]
            for r in range(1, nt):
                summed = summed + pr[par, r - 1].astype(jnp.float32)
            update = (summed * scale).astype(jnp.bfloat16)
            new = (xs[d].astype(jnp.float32) + update.astype(jnp.float32)).astype(jnp.bfloat16)
            if j + 1 == LAYERS:
                fin[...] = new
                return
            givers = [i for i in act if i + 1 < ns and first[i + 1] <= j + 1 <= last[i + 1]]
            stay = [i for i in act if j + 1 < end[i]]

            def xcopy(k):
                return rcopy(
                    xr.at[nxt, d], xr.at[nxt, d], xs_ss.at[k - 1], xr_rs.at[nxt, k - 1], dp=dp_of(k)
                )

            if stay:
                @pl.when(among(s, stay))
                def _():
                    xr[nxt, d] = new
                    for k in range(1, nd):
                        xcopy(k).start()
            if givers:
                @pl.when(among(s, givers))
                def _():
                    give_id = pick(s, [j + 1 - first[i + 1] if i in givers else 0 for i in range(ns)])
                    hst[give_id] = new
                    for k in range(nd):
                        rcopy(
                            hst.at[give_id], hr.at[give_id, d], h_ss.at[give_id, k],
                            h_rs.at[give_id, k], dp=dp_of(k), section=s + 1,
                        ).start()
            if stay:
                @pl.when(among(s, stay))
                def _():
                    for k in range(1, nd):
                        xcopy(k).wait()

    for j in range(LAYERS):
        layer(j)

    top = ns - 1

    def cocopy(kt):
        return rcopy(fin, cout, co_ss.at[kt], co_rs, section=t, tensor=tq_of(kt))

    def bocopy(sec, kd):
        to = dp_of(kd)
        part = pl.ds(pl.multiple_of(to * tl, tl), tl)
        return rcopy(
            fin.at[part, :], bo.at[d], bo_ss.at[sec, kd], bo_rs.at[kd], dp=to, section=sec
        )

    outs = [(sec, kd) for sec in range(ns) for kd in range(nd) if sec != top or kd]

    @pl.when(s == top)
    def _():
        for kt in range(1, nt):
            cocopy(kt).start()

        @pl.when(t != top)
        def _():
            cocopy(0).start()

        @pl.when(t == top)
        def _():
            cout[...] = fin[...]

        for sec, kd in outs:
            bocopy(sec, kd).start()
        bo[d] = fin[mine, :]

    for i in range(ns):
        @pl.when(s == i)
        def _(i=i):
            for k in range(slots):
                if k not in waited[i]:
                    for r in range(1, nt + 1):
                        wcopy(k, r).wait()
            if i + 1 < ns:
                for h in range(last[i + 1] - first[i + 1] + 1):
                    for kd in range(nd):
                        rcopy(
                            hst.at[h], hr.at[h, d], h_ss.at[h, kd], h_rs.at[h, kd]
                        ).wait_send()

    @pl.when(t == s)
    def _():
        for kt, kd in pairs:
            cicopy(kt, kd).wait_send()
        for kd in range(1, nd):
            cicopy(1, kd).wait_recv()

    @pl.when(t != s)
    def _():
        for kd in range(nd):
            cicopy(1, kd).wait_recv()

    for b in range(nb):
        rows_out[:, b * q:(b + 1) * q] = x0r[b]
    cin_out[...] = cin[...]

    @pl.when((s != top) | (t != top))
    def _():
        cocopy(1).wait_recv()

    cout_out[...] = cout[...]

    @pl.when(s != top)
    def _():
        for kd in range(nd):
            bocopy(0, kd).wait_recv()

    @pl.when(s == top)
    def _():
        for kd in range(1, nd):
            bocopy(0, kd).wait_recv()
        for kt in range(1, nt):
            cocopy(kt).wait_send()

        @pl.when(t != top)
        def _():
            cocopy(0).wait_send()

        for sec, kd in outs:
            bocopy(sec, kd).wait_send()

    bo_out[...] = bo[...]


def local(nd, ns, nt, block_in, weights, gains, layer_counts):
    tl, nb, q = block_in.shape
    slots, _, _, width = weights.shape
    assert nb == nd and width == nt * q and ns == nt
    T, K = tl * nd, nb * q
    first, last, _ = windows(ns, slots)
    hands = max(last[i] - first[i] + 1 for i in range(1, ns))
    bf, f32 = jnp.bfloat16, jnp.float32
    DMA = pltpu.SemaphoreType.DMA
    vm = pl.BlockSpec(memory_space=pltpu.VMEM)
    rows, cols_in, cols_out, out = pl.pallas_call(
        functools.partial(relay, nd, ns, nt, slots),
        out_shape=(
            jax.ShapeDtypeStruct((T, K), bf),
            jax.ShapeDtypeStruct((T, q), bf),
            jax.ShapeDtypeStruct((T, q), bf),
            jax.ShapeDtypeStruct((nb, tl, q), bf),
        ),
        in_specs=[
            pl.BlockSpec(memory_space=pltpu.SMEM), vm, vm, pl.BlockSpec(memory_space=pl.ANY),
        ],
        out_specs=(vm, vm, vm, vm),
        scratch_shapes=[
            pltpu.VMEM((slots, K, width), bf),
            pltpu.VMEM((nb, T, q), bf),
            pltpu.VMEM((2, nb, T, q), bf),
            pltpu.VMEM((hands, nb, T, q), bf),
            pltpu.VMEM((hands, T, q), bf),
            pltpu.VMEM((nb, T, q), bf),
            pltpu.VMEM((T, K), bf),
            pltpu.VMEM((nt - 1, T, q), bf),
            pltpu.VMEM((2, nt - 1, T, q), bf),
            pltpu.VMEM((T, q), f32),
            pltpu.VMEM((T, 128), f32),
            pltpu.VMEM((2, nt - 1, T, 128), f32),
            pltpu.VMEM((T, q), bf),
            pltpu.VMEM((T, q), bf),
            pltpu.VMEM((T, q), bf),
            pltpu.VMEM((nb, tl, q), bf),
            DMA((slots, nt)), DMA((max(nd - 1, 1),)), DMA((max(nd - 1, 1),)), DMA, DMA((nd,)),
            DMA((nt - 1,)), DMA((2, nt - 1)), DMA((nt - 1,)), DMA((2, nt - 1)),
            DMA((max(nd - 1, 1),)), DMA((2, max(nd - 1, 1))), DMA((hands, nd)), DMA((hands, nd)),
            DMA((nt,)), DMA, DMA((ns, nd)), DMA((nd,)),
        ],
        compiler_params=pltpu.CompilerParams(
            collective_id=0, has_side_effects=True, vmem_limit_bytes=VMEM_LIMIT
        ),
    )(
        layer_counts, block_in.transpose(1, 0, 2), gains.reshape(slots, 1, K),
        weights.reshape(slots, K, width),
    )
    contract = (((0,), (0,)), ((), ()))
    gram_in = lax.dot_general(rows, cols_in, contract, preferred_element_type=f32) / T
    gram_cross = lax.dot_general(rows, cols_out, contract, preferred_element_type=f32) / T
    return (
        out.transpose(1, 0, 2),
        gram_in.reshape(nb, q, 1, q),
        gram_cross.reshape(nb, q, 1, q),
    )


def solution(mesh):
    nd, ns, nt = mesh.shape["dp"], mesh.shape["section"], mesh.shape["tensor"]
    return jax.shard_map(
        functools.partial(local, nd, ns, nt),
        mesh=mesh,
        in_specs=(
            P("dp", None, "tensor"),
            P("section", None, "tensor", "dp"),
            P("section", None, "tensor"),
            P(),
        ),
        out_specs=(
            P("dp", None, "tensor"),
            P(None, "tensor", "dp", "section"),
            P(None, "tensor", "dp", "section"),
        ),
        check_vma=False,
    )
```

time: 1880 us -> 199 us (0.11)
  local copies, waits for them, and re-layouts: 664 us -> 37.2 us
  waiting for transfers between devices: 493 us -> 0 us
  blocking collectives: 322 us -> 0 us
  matrix products: 239 us -> 3.52 us
  Pallas kernels: 0 us -> 158 us
  starting transfers between devices: 84.5 us -> 0 us
  other arithmetic: 35.8 us -> 0 us
    reduce_scatter x21 -> x0, waiting for transfers between devices: 403 us -> none  [apply_layer(): lax.psum_scatter(product.reshape(block_count * all_rows, piece_width), 't...]
    while x64 -> x0, local copies, waits for them, and re-layouts: 316 us -> none
    dynamic_slice x22 -> x0, local copies, waits for them, and re-layouts: 278 us -> none  [the longest x21 278 us: one_layer(): return apply_layer(current, weights[slot_id], gains[slot_id])]
    dot_general x23 -> x2, matrix products: 239 us -> 3.52 us  [the longest x1 2.25 us: local(): lax.dot_general(rows, cols_in, contract, preferred_element_type=f32) / T]
    psum x21 -> x0, blocking collectives: 189 us -> none  [apply_layer(): squares = lax.psum(jnp.sum(wide_rows * wide_rows, axis=1), 'tensor')]
    pallas_call x0 -> x1, Pallas kernels: none -> 158 us  [local(): pl.pallas_call(functools.partial(relay, nd, ns, nt, slots), out_shape=(ja...]
    all_gather x24 -> x0, blocking collectives: 133 us -> none  [the longest x21 96.1 us: apply_layer(): gathered = lax.all_gather(normed, 'dp', axis=0, tiled=True)]
    all_to_all x23 -> x0, starting transfers between devices: 75.2 us -> none  [the longest x21 68.4 us: apply_layer(): lax.all_to_all(update, 'dp', split_axis=0, concat_axis=2, tiled=True)]
  transfers between devices with their start and end apart: 51 -> 0, of which waited for: 49 -> 0; matrix products, arithmetic and copies ran while one was open for 2% -> 0% of each run, Pallas kernels for 0% -> 0%
where the time goes in v1:
time: 199 us
  Pallas kernels  158 us (79%)
  local copies, waits for them, and re-layouts  37.2 us (19%)
  matrix products  3.52 us (2%)
    pallas_call x1, Pallas kernels, local(): pl.pallas_call(functools.partial(relay, nd, ns, nt, slots), out_shape=(ja...  158 us
    unnamed x8, local copies, waits for them, and re-layouts  35.8 us

profile of v1, /device:TPU:0, one launch (start us, length us, event | category | flops | bytes accessed | tf_op | source)
XLA Modules:
  0.0 199.2 jit_solution(1994210623994772804)
XLA Ops:
  0.6 1.4 reshape.18.gains
  2.0 1.6 copy.12
  3.6 157.8 %shard_map.67 = (bf16[64,2048]{1,0:T(8,128)(2,1)}, bf16[64,1024]{1,0:T(8,128)(2,1)}, bf16[64,1024]{1,0:T(8,128)(2,1)}, bf16[2,32,1024]{2,1,0:T(8,128)(2,1)}) custom-call(s32[4]{0:T(128)} %counts.1, bf16[2,32,1024]{2,1,0:T(8,128)(2,1)} %bitcast.14, f32[3,1,2048]{2,1,0:T(1,128)} %reshape.18.gains, bf16[3,2048,4096]{2,1,0:T(8,128)(2,1)} %bitcast.13), custom_call_target="tpu_custom_call" | custom-call | tf_op jit(solution)/shard_map/pallas_call | solution.py:359
  161.4 1.7 copy.8
  163.1 2.3 %convolution_multiply_fusion.1 = f32[2048,1024]{1,0:T(8,128)S(1)} fusion(bf16[64,2048]{1,0:T(8,128)(2,1)} %get-tuple-element.8, bf16[64,1024]{1,0:T(8,128)(2,1)} %get-tuple-element.9), kind=kOutput, calls=%fused_computation.1 | convolution fusion | flops 270532608 | bytes 8781824 | tf_op jit(solution)/shard_map/dot_general | solution.py:401
  165.3 0.0 copy-start
  165.3 0.0 copy-start.1
  165.4 16.3 %copy.9 = f32[2,1024,1,1024]{3,2,1,0:T(1,128)} copy(f32[2,1024,1,1024]{3,1,0,2:T(8,128)S(1)} %bitcast.12) | data formatting | bytes 16777216
  181.6 0.0 copy-done
  181.6 0.0 copy-done.1
  181.6 1.3 convolution_multiply_fusion
  182.9 16.3 %copy.10 = f32[2,1024,1,1024]{3,2,1,0:T(1,128)} copy(f32[2,1024,1,1024]{3,1,0,2:T(8,128)S(1)} %bitcast.11) | data formatting | bytes 16777216
Async XLA Ops:
  165.3 16.3 %copy-start = (bf16[64,2048]{1,0:T(8,128)(2,1)S(1)}, bf16[64,2048]{1,0:T(8,128)(2,1)}, u32[]{:S(2)}) copy-start(bf16[64,2048]{1,0:T(8,128)(2,1)} %get-tuple-element.8) | copy-start | bytes 786436
  165.3 16.3 %copy-start.1 = (bf16[64,1024]{1,0:T(8,128)(2,1)S(1)}, bf16[64,1024]{1,0:T(8,128)(2,1)}, u32[]{:S(2)}) copy-start(bf16[64,1024]{1,0:T(8,128)(2,1)} %get-tuple-element.10) | copy-start | bytes 393220
